TPU v7x, 256 devices: a whole 4x4x8 slice. The times are simulated.
256 devices in a mesh: samp: 8 (over y, core), par: 32 (over z, x).
Axes of the slice: x: 4, y: 4, z: 8, core: 2. Of those that a mesh axis runs over, the one named last changes fastest.
Arguments:
- jacobian: bfloat16 [8192, 65536], P(('samp', 'par')), as said below
- sample_slot: int32 [8192], P(('samp', 'par')), may hold values from 0 to 1023, as said below
- panel_index: int32 [1], replicated, may hold values from 0 to 8191
- shift_value: float32 [1], replicated, may hold values from 0.1 to 1
Outputs:
- cholesky_panel: float32 [8192, 1024], P(('samp', 'par'))
Inputs may be any that keep to these rules, and one draw needn't show every extreme that they name: Within each group (samples g * 1024 to (g + 1) * 1024 - 1), sample_slot is a permutation of 0 to 1023. `jacobian`: finite values.
All inputs are finite; a program needn't handle non-finite values.
Results may differ from a plain program's by a relative error of at most 0.0003.
Values may be sent and summed in bfloat16 or wider, within the bound.
A program may use at most 128 MiB of HBM per device.

v0:
```python
import jax
import jax.numpy as jnp
from jax import lax
from jax.sharding import Mesh
from jax.sharding import PartitionSpec as P

PAR = ("par_0", "par_1")
SAMP_PAR = ("samp", "par_0", "par_1")


def sent_to_all(shard, axis):
    peers = lax.axis_size(axis)
    return lax.all_to_all(
        jnp.broadcast_to(shard[None], (peers, *shard.shape)), axis, 0, 0, tiled=True
    )


def laid_out(tiles, dim):
    tiles = jnp.moveaxis(tiles, 0, dim)
    dims = tiles.shape
    return tiles.reshape(*dims[:dim], dims[dim] * dims[dim + 1], *dims[dim + 2 :])


def gather_directly(shard, axis, dim):
    tiles = sent_to_all(shard, axis)
    return laid_out(tiles, dim)


def padded_to(lines, peers):
    spare = -len(lines) % peers
    return jnp.pad(lines, [(0, spare)] + [(0, 0)] * (lines.ndim - 1))


def spread(shard, axis, root):
    lines = jnp.where(lax.axis_index(axis) == root, shard, jnp.zeros_like(shard)).reshape(
        -1, *shard.shape[1:][-1:]
    )
    padded = padded_to(lines, lax.axis_size(axis))
    own = lax.psum_scatter(padded, axis, scatter_dimension=0, tiled=True)
    return lax.all_gather(own, axis, axis=0, tiled=True)[: len(lines)].reshape(shard.shape)


def sum_by_axis(shard, axes, dim):
    if not axes:
        return shard
    nearer = lax.psum_scatter(shard, axes[0], scatter_dimension=dim, tiled=True)
    return sum_by_axis(nearer, axes[1:], dim)


def invert_factor(block, identity_matrix):
    factor = jnp.linalg.cholesky(block)
    return lax.linalg.triangular_solve(factor, identity_matrix, left_side=True, lower=True)


def on_device(jacobian, sample_slot, panel_index, shift_value):
    arrived = lax.all_to_all(jacobian, PAR, split_axis=1, concat_axis=0, tiled=True)
    own_slots = gather_directly(sample_slot, PAR, 0)
    inverse = jnp.argsort(own_slots)
    ordered = jnp.take(arrived, inverse, axis=0)
    group_width = ordered.shape[0]
    pivot_group = panel_index[0] // group_width
    rotation = panel_index[0] % group_width
    pivot_rows = jnp.roll(spread(ordered, "samp", pivot_group), -rotation, axis=0)
    partial_gram = lax.dot_general(
        ordered, pivot_rows, (((1,), (1,)), ((), ())), preferred_element_type=jnp.float32
    )
    share = group_width // lax.axis_size(PAR)
    samples = group_width * lax.axis_size("samp")
    identity_matrix = jnp.eye(group_width, dtype=jnp.float32)
    shifted_eye = jnp.roll(identity_matrix, -rotation, axis=1)
    on_pivot = (lax.axis_index("samp") == pivot_group).astype(jnp.float32)
    shift_term = shift_value[0] * on_pivot
    start = lax.axis_index(PAR) * share
    summed = sum_by_axis(partial_gram, PAR, 0)
    band = lax.dynamic_slice_in_dim(shifted_eye, start, share, 0)
    my_rows = summed / samples + shift_term * band
    pivot_partial = lax.dot_general(
        pivot_rows, pivot_rows, (((1,), (1,)), ((), ())), preferred_element_type=jnp.float32
    )
    pivot_sum = lax.psum(pivot_partial, PAR)
    pivot_block = pivot_sum / samples + shift_value[0] * identity_matrix
    inverse_factor = invert_factor(pivot_block, identity_matrix)
    return lax.dot_general(
        my_rows,
        inverse_factor,
        (((1,), (1,)), ((), ())),
        precision=lax.Precision.HIGHEST,
        preferred_element_type=jnp.float32,
    )


def solution(mesh):
    torus = Mesh(mesh.devices.reshape(mesh.shape["samp"], 8, 4), ("samp", "par_0", "par_1"))
    return jax.shard_map(
        on_device,
        mesh=torus,
        in_specs=(P(SAMP_PAR, None), P(SAMP_PAR), P(), P()),
        out_specs=P(SAMP_PAR, None),
        check_vma=False,
    )
```

profile of v0, /device:TPU:8, one launch (start us, length us, event | category | flops | bytes accessed | tf_op | source)
XLA Modules:
  0.0 796.8 jit_solution(5502740099929445992)
XLA Ops:
  7.8 11.3 %all-to-all-start = ((s32[32,1,32]{2,1,0:T(1,128)}), s32[32,1,32]{2,1,0:T(1,128)S(1)}, u32[]{:S(2)}, u32[]{:S(2)}) async-start(s32[32,1,32]{2,1,0:T(1,128)} %broadcast_in_dim.23), calls=%async_computation | async-start | bytes 32768 | tf_op jit(solution)/shard_map/all_to_all | solution.py:13
  19.1 4.7 copy.55
  23.9 4.9 all-to-all-done
  28.8 5.0 all-to-all-start.1
  35.8 4.4 sort.17
  40.2 87.4 %all-to-all-done.1 = bf16[32,32,2048]{2,0,1:T(8,128)(2,1)} async-done(((bf16[32,32,2048]{2,0,1:T(8,128)(2,1)}), bf16[32,32,2048]{2,0,1:T(8,128)(2,1)}, u32[]{:S(2)}, u32[]{:S(2)}) %all-to-all-start.1) | async-done | bytes 4194336 | tf_op jit(solution)/shard_map/all_to_all | solution.py:56
  127.6 11.6 %gather_fusion = bf16[1024,2048]{1,0:T(8,128)(2,1)} fusion(bf16[1024,2048]{1,0:T(8,128)(2,1)} %bitcast.1, s32[1024]{0:T(1024)S(1)} %fusion.77), kind=kCustom, calls=%fused_computation | custom fusion | bytes 8392704 | tf_op jit(solution)/shard_map/jit(_take)/gather | solution.py:59
  139.2 4.0 broadcast_select_fusion.1
  143.2 35.1 %reduce-scatter.6.cloned.1.call-done = bf16[128,2048]{1,0:T(8,128)(2,1)} async-done(((bf16[1024,2048]{1,0:T(8,128)(2,1)}), bf16[128,2048]{1,0:T(8,128)(2,1)}) %reduce-scatter.6.cloned.1.call-update) | async-done | bytes 524304 | tf_op jit(solution)/shard_map/reduce_scatter | solution.py:39
  178.4 37.8 %all-gather.2.cloned.1.call-done = bf16[1024,2048]{1,0:T(8,128)(2,1)} async-done(((bf16[128,2048]{1,0:T(8,128)(2,1)}), bf16[1024,2048]{1,0:T(8,128)(2,1)}) %all-gather.2.cloned.1.call-update) | async-done | bytes 4194320 | tf_op jit(solution)/shard_map/all_gather | solution.py:40
  216.2 13.5 %fusion.85 = f32[1024,1024]{0,1:T(8,128)} fusion(s32[]{:T(128)S(6)} %select_n.64, bf16[1024,2048]{1,0:T(8,128)(2,1)} %all-gather.2.cloned.1.call-done), kind=kOutput, calls=%fused_computation.182 | convolution fusion | flops 4303355904 | bytes 8388612 | tf_op jit(solution)/shard_map/dot_general | solution.py:77
  232.0 2.4 fusion.2
  234.4 9.8 %fusion.11 = f32[1024,1024]{0,1:T(8,128)} fusion(bf16[1024,2048]{1,0:T(8,128)(2,1)S(1)} %copy-done.2, pred[1024]{0:T(1024)(128)(4,1)S(1)} %compare_and_fusion, s32[]{:T(128)S(6)} %select_n.64, bf16[1024,2048]{1,0:T(8,128)(2,1)} %all-gather.2.cloned.1.call-done), kind=kOutput, calls=%fused_computation.26 | convolution fusion | flops 4305453056 | bytes 12583940 | tf_op jit(solution)/shard_map/dot_general | solution.py:64
  244.3 150.8 %all-reduce.3.cloned.1.call-done = f32[1024,1024]{0,1:T(8,128)} async-done(((f32[1024,1024]{0,1:T(8,128)}), f32[1024,1024]{0,1:T(8,128)}) %all-reduce.3.cloned.1.call-update) | async-done | bytes 4194320 | tf_op jit(solution)/shard_map/psum | solution.py:80
  395.1 5.0 select_add_fusion
  400.1 5.4 copy.26
  405.5 4.7 fusion.1
  410.2 2.0 copy-done.3
  412.2 11.7 %cholesky.222 = f32[128,128]{1,0:T(8,128)S(1)} custom-call(f32[128,128]{1,0:T(8,128)S(1)} %cholesky.577), custom_call_target="Cholesky" | custom-call | tf_op jit(solution)/shard_map/jit(cholesky)/cholesky | solution.py:51
  424.1 9.8 %custom-call.62 = f32[1,128,128]{1,2,0:T(8,128)S(1)} custom-call(f32[1,128,128]{2,1,0:T(8,128)S(1)} %get-tuple-element.71), custom_call_target="InvertDiagBlocksLowerTriangular" | custom-call | tf_op jit(solution)/shard_map/jit(cholesky)/cholesky | solution.py:51
  437.2 11.7 %cholesky.243 = f32[128,128]{1,0:T(8,128)S(1)} custom-call(f32[128,128]{1,0:T(8,128)S(1)} %cholesky.581), custom_call_target="Cholesky" | custom-call | tf_op jit(solution)/shard_map/jit(cholesky)/cholesky | solution.py:51
  449.4 9.8 %custom-call.63 = f32[1,128,128]{1,2,0:T(8,128)S(1)} custom-call(f32[1,128,128]{2,1,0:T(8,128)S(1)} %get-tuple-element.69), custom_call_target="InvertDiagBlocksLowerTriangular" | custom-call | tf_op jit(solution)/shard_map/jit(cholesky)/cholesky | solution.py:51
  460.4 1.9 copy-done
  462.3 2.4 convolution_subtract_fusion.6
  464.7 11.7 %cholesky.466 = f32[128,128]{1,0:T(8,128)S(1)} custom-call(f32[128,128]{1,0:T(8,128)S(1)} %cholesky.586), custom_call_target="Cholesky" | custom-call | tf_op jit(solution)/shard_map/jit(cholesky)/cholesky | solution.py:51
  477.2 9.8 %custom-call.64 = f32[1,128,128]{1,2,0:T(8,128)S(1)} custom-call(f32[1,128,128]{2,1,0:T(8,128)S(1)} %get-tuple-element.67), custom_call_target="InvertDiagBlocksLowerTriangular" | custom-call | tf_op jit(solution)/shard_map/jit(cholesky)/cholesky | solution.py:51
  488.3 3.3 convolution_subtract_fusion.7
  491.6 11.7 %cholesky.485 = f32[128,128]{1,0:T(8,128)S(1)} custom-call(f32[128,128]{1,0:T(8,128)S(1)} %cholesky.591), custom_call_target="Cholesky" | custom-call | tf_op jit(solution)/shard_map/jit(cholesky)/cholesky | solution.py:51
  504.1 9.8 %custom-call.65 = f32[1,128,128]{1,2,0:T(8,128)S(1)} custom-call(f32[1,128,128]{2,1,0:T(8,128)S(1)} %get-tuple-element.65), custom_call_target="InvertDiagBlocksLowerTriangular" | custom-call | tf_op jit(solution)/shard_map/jit(cholesky)/cholesky | solution.py:51
  515.0 3.2 convolution_subtract_fusion.8
  518.2 12.1 %cholesky.504 = f32[128,128]{1,0:T(8,128)S(1)} custom-call(f32[128,128]{1,0:T(8,128)S(1)} %cholesky.596), custom_call_target="Cholesky" | custom-call | tf_op jit(solution)/shard_map/jit(cholesky)/cholesky | solution.py:51
  531.1 9.8 %custom-call.66 = f32[1,128,128]{1,2,0:T(8,128)S(1)} custom-call(f32[1,128,128]{2,1,0:T(8,128)S(1)} %get-tuple-element.63), custom_call_target="InvertDiagBlocksLowerTriangular" | custom-call | tf_op jit(solution)/shard_map/jit(cholesky)/cholesky | solution.py:51
  542.0 3.1 convolution_subtract_fusion.9
  545.1 11.7 %cholesky.524 = f32[128,128]{1,0:T(8,128)S(1)} custom-call(f32[128,128]{1,0:T(8,128)S(1)} %cholesky.601), custom_call_target="Cholesky" | custom-call | tf_op jit(solution)/shard_map/jit(cholesky)/cholesky | solution.py:51
  557.6 9.8 %custom-call.67 = f32[1,128,128]{1,2,0:T(8,128)S(1)} custom-call(f32[1,128,128]{2,1,0:T(8,128)S(1)} %get-tuple-element.61), custom_call_target="InvertDiagBlocksLowerTriangular" | custom-call | tf_op jit(solution)/shard_map/jit(cholesky)/cholesky | solution.py:51
  568.4 2.8 convolution_subtract_fusion.10
  571.3 11.7 %cholesky.544 = f32[128,128]{1,0:T(8,128)S(1)} custom-call(f32[128,128]{1,0:T(8,128)S(1)} %cholesky.606), custom_call_target="Cholesky" | custom-call | tf_op jit(solution)/shard_map/jit(cholesky)/cholesky | solution.py:51
  583.8 9.8 %custom-call.68 = f32[1,128,128]{1,2,0:T(8,128)S(1)} custom-call(f32[1,128,128]{2,1,0:T(8,128)S(1)} %get-tuple-element.59), custom_call_target="InvertDiagBlocksLowerTriangular" | custom-call | tf_op jit(solution)/shard_map/jit(cholesky)/cholesky | solution.py:51
  594.5 2.1 convolution_subtract_fusion.11
  596.6 11.7 %cholesky.562 = f32[128,128]{1,0:T(8,128)S(1)} custom-call(f32[128,128]{1,0:T(8,128)S(1)} %convolution_subtract_fusion.11), custom_call_target="Cholesky" | custom-call | tf_op jit(solution)/shard_map/jit(cholesky)/cholesky | solution.py:51
  618.7 4.9 select_select_fusion
  623.5 24.0 %while.1 = (s32[]{:T(128)}, f32[1024,1024]{0,1:T(8,128)}, s32[8,2]{0,1:T(2,128)S(1)}, f32[8,128,128]{2,1,0:T(8,128)S(1)}, s32[]{:T(128)}) while((s32[]{:T(128)}, f32[1024,1024]{0,1:T(8,128)}, s32[8,2]{0,1:T(2,128)S(1)}, f32[8,128,128]{2,1,0:T(8,128)S(1)}, s32[]{:T(128)}) %tuple.51), condition=%wide.while_cond, body=%wide.while_body.sunk | while | flops 2 | bytes 393329 | solution.py:52
  624.2 2.3 dynamic-slice.7
  627.2 2.3 dynamic-slice.7
  630.2 2.3 dynamic-slice.7
  633.2 2.3 dynamic-slice.7
  636.2 2.3 dynamic-slice.7
  639.2 2.3 dynamic-slice.7
  642.2 2.3 dynamic-slice.7
  645.2 2.2 dynamic-slice.7
  647.5 79.6 %custom-call.69 = f32[8,128,128]{1,2,0:T(8,128)} custom-call(f32[8,128,128]{2,1,0:T(8,128)S(1)} %get-tuple-element.14), custom_call_target="InvertDiagBlocksLowerTriangular" | custom-call | tf_op jit(solution)/shard_map/triangular_solve | solution.py:52
  727.1 2.5 constant_dynamic-update-slice_fusion.17
  729.7 2.1 convolution_subtract_fusion.4
  731.8 2.7 constant_dynamic-update-slice_fusion.16
  734.5 2.7 convolution_subtract_fusion
  739.0 3.7 fusion.18
  744.5 4.4 fusion.21
  750.9 5.4 convolution_subtract_fusion.2
  758.0 2.0 copy.50
  760.1 6.2 convolution_subtract_fusion.1
  766.3 2.5 constant_dynamic-update-slice_fusion.11
  768.8 8.5 %convolution_subtract_fusion.3 = f32[128,1024]{0,1:T(8,128)S(1)} fusion(f32[896,1024]{1,0:T(8,128)} %get-tuple-element.33, f32[1024,1024]{0,1:T(8,128)} %fusion.2, f32[1024,1024]{0,1:T(8,128)} %get-tuple-element.132), kind=kOutput, calls=%fused_computation.40 | convolution fusion | flops 1409417216 | bytes 5177344 | tf_op jit(solution)/shard_map/triangular_solve | solution.py:52
  777.3 2.3 convolution_dynamic-update-slice_fusion
  782.4 7.6 fusion.33
  (116 shorter events, 39.6 us)
Async XLA Ops:
  7.8 21.0 %all-to-all-start = ((s32[32,1,32]{2,1,0:T(1,128)}), s32[32,1,32]{2,1,0:T(1,128)S(1)}, u32[]{:S(2)}, u32[]{:S(2)}) async-start(s32[32,1,32]{2,1,0:T(1,128)} %broadcast_in_dim.23), calls=%async_computation | async-start | bytes 32768 | tf_op jit(solution)/shard_map/all_to_all | solution.py:13
  28.8 98.8 %all-to-all-start.1 = ((bf16[32,32,2048]{2,0,1:T(8,128)(2,1)}), bf16[32,32,2048]{2,0,1:T(8,128)(2,1)}, u32[]{:S(2)}, u32[]{:S(2)}) async-start(bf16[32,32,2048]{2,0,1:T(8,128)(2,1)} %bitcast.117), calls=%async_computation.1 | async-start | bytes 8388608 | tf_op jit(solution)/shard_map/all_to_all | solution.py:56
  33.8 144.5 %reduce-scatter.6.cloned.1.call-start = ((), (), s32[]{:S(2)}) async-start(), calls=%async_computation.5 | async-start | bytes 4718592 | tf_op jit(solution)/shard_map/reduce_scatter | solution.py:39
  143.1 73.1 %all-gather.2.cloned.1.call-start = ((), (), s32[]{:S(2)}) async-start(), calls=%async_computation.6 | async-start | bytes 4718592 | tf_op jit(solution)/shard_map/all_gather | solution.py:40
  178.4 216.8 %all-reduce.3.cloned.1.call-start = ((), (), s32[]{:S(2)}) async-start(), calls=%async_computation.8 | async-start | bytes 8388608 | tf_op jit(solution)/shard_map/psum | solution.py:80
  229.7 528.2 %reduce-scatter.8.cloned.1.call-start = ((), (), s32[]{:S(2)}) async-start(), calls=%async_computation.7 | async-start | bytes 4718592 | tf_op jit(solution)/shard_map/reduce_scatter | solution.py:46
  230.7 3.7 copy-start.2
  244.3 537.1 %reduce-scatter.10.cloned.1.call-start = ((), (), s32[]{:S(2)}) async-start(), calls=%async_computation.9 | async-start | bytes 655360
  410.2 2.0 copy-start.3
  460.3 2.0 copy-start
  727.1 7.4 copy-start.1
  729.7 7.6 copy-start.4
Sparse Core Ops, SparseCore 0:
  143.3 35.0 reduce-scatter.5
  180.2 35.9 all-gather.1
  229.9 165.2 all-reduce.2
  397.5 52.5 reduce-scatter.7
  760.2 21.1 reduce-scatter.9
where the time goes:
time: 806 us; the launch traced here: 797 us
  waiting for transfers between devices  318 us (39%)
  other arithmetic  274 us (34%)
  matrix products  107 us (13%)
  local copies, waits for them, and re-layouts  60.1 us (7%)
  between operations  20.3 us (3%)
  starting transfers between devices  16.7 us (2%)
    another operation x30, other arithmetic, invert_factor(): factor = jnp.linalg.cholesky(block)  167 us
    psum x1, waiting for transfers between devices, on_device(): pivot_sum = lax.psum(pivot_partial, PAR)  151 us
    all_to_all x1, waiting for transfers between devices, on_device(): lax.all_to_all(jacobian, PAR, split_axis=1, concat_axis=0, tiled=True)  87.4 us
    another operation x3, other arithmetic, invert_factor(): lax.linalg.triangular_solve(factor, identity_matrix, left_side=True, lowe...  84.5 us
    another operation x15, matrix products, invert_factor(): lax.linalg.triangular_solve(factor, identity_matrix, left_side=True, lowe...  50.3 us
    all_gather x1, waiting for transfers between devices, spread(): lax.all_gather(own, axis, axis=0, tiled=True)[:len(lines)]  37.8 us
    reduce_scatter x1, waiting for transfers between devices, spread(): own = lax.psum_scatter(padded, axis, scatter_dimension=0, tiled=True)  35.1 us
    another operation x14, matrix products, invert_factor(): factor = jnp.linalg.cholesky(block)  25.9 us
  transfers between devices with their start and end apart: 7, of which 6 were waited for; matrix products, arithmetic and copies ran while one was open for 50% of the time, Pallas kernels for 0%

commit v1 on v0

--- a/solution.py
+++ b/solution.py
@@ -77,7 +77,7 @@
     pivot_partial = lax.dot_general(
         pivot_rows, pivot_rows, (((1,), (1,)), ((), ())), preferred_element_type=jnp.float32
     )
-    pivot_sum = lax.psum(pivot_partial, PAR)
+    pivot_sum = lax.psum(lax.psum(pivot_partial, "par_0"), "par_1")
     pivot_block = pivot_sum / samples + shift_value[0] * identity_matrix
     inverse_factor = invert_factor(pivot_block, identity_matrix)
     return lax.dot_general(

time: 806 us -> 853 us (1.058)
  waiting for transfers between devices: 318 us -> 364 us
    psum x1 -> x2, waiting for transfers between devices: 151 us -> 194 us  [on_device(): pivot_sum = lax.psum(lax.psum(pivot_partial, 'par_0'), 'par_1')]
  transfers between devices with their start and end apart: 7 -> 8, of which waited for: 6 -> 7; matrix products, arithmetic and copies ran while one was open for 50% -> 47% of each run, Pallas kernels for 0% -> 0%
where the time goes in v1:
time: 853 us; the launch traced here: 843 us
  waiting for transfers between devices  364 us (43%)
  other arithmetic  274 us (32%)
  matrix products  107 us (13%)
  local copies, waits for them, and re-layouts  60.1 us (7%)
  between operations  20.6 us (2%)
  starting transfers between devices  16.7 us (2%)
    psum x2, waiting for transfers between devices, on_device(): pivot_sum = lax.psum(lax.psum(pivot_partial, 'par_0'), 'par_1')  194 us
    another operation x30, other arithmetic, invert_factor(): factor = jnp.linalg.cholesky(block)  167 us
    all_to_all x1, waiting for transfers between devices, on_device(): lax.all_to_all(jacobian, PAR, split_axis=1, concat_axis=0, tiled=True)  87.4 us
    another operation x3, other arithmetic, invert_factor(): lax.linalg.triangular_solve(factor, identity_matrix, left_side=True, lowe...  84.5 us
    another operation x15, matrix products, invert_factor(): lax.linalg.triangular_solve(factor, identity_matrix, left_side=True, lowe...  50.3 us
    all_gather x1, waiting for transfers between devices, spread(): lax.all_gather(own, axis, axis=0, tiled=True)[:len(lines)]  37.8 us
    reduce_scatter x1, waiting for transfers between devices, spread(): own = lax.psum_scatter(padded, axis, scatter_dimension=0, tiled=True)  35.1 us
    another operation x14, matrix products, invert_factor(): factor = jnp.linalg.cholesky(block)  25.9 us
  transfers between devices with their start and end apart: 8, of which 7 were waited for; matrix products, arithmetic and copies ran while one was open for 47% of the time, Pallas kernels for 0%

profile of v1, /device:TPU:8, one launch (start us, length us, event | category | flops | bytes accessed | tf_op | source)
XLA Modules:
  0.0 843.3 jit_solution(17203489413983541085)
XLA Ops:
  7.8 11.3 %all-to-all-start = ((s32[32,1,32]{2,1,0:T(1,128)}), s32[32,1,32]{2,1,0:T(1,128)S(1)}, u32[]{:S(2)}, u32[]{:S(2)}) async-start(s32[32,1,32]{2,1,0:T(1,128)} %broadcast_in_dim.23), calls=%async_computation | async-start | bytes 32768 | tf_op jit(solution)/shard_map/all_to_all | solution.py:13
  19.1 4.7 copy.55
  23.9 4.9 all-to-all-done
  28.8 5.0 all-to-all-start.1
  35.8 4.4 sort.17
  40.2 87.4 %all-to-all-done.1 = bf16[32,32,2048]{2,0,1:T(8,128)(2,1)} async-done(((bf16[32,32,2048]{2,0,1:T(8,128)(2,1)}), bf16[32,32,2048]{2,0,1:T(8,128)(2,1)}, u32[]{:S(2)}, u32[]{:S(2)}) %all-to-all-start.1) | async-done | bytes 4194336 | tf_op jit(solution)/shard_map/all_to_all | solution.py:56
  127.6 11.6 %gather_fusion = bf16[1024,2048]{1,0:T(8,128)(2,1)} fusion(bf16[1024,2048]{1,0:T(8,128)(2,1)} %bitcast.1, s32[1024]{0:T(1024)S(1)} %fusion.77), kind=kCustom, calls=%fused_computation | custom fusion | bytes 8392704 | tf_op jit(solution)/shard_map/jit(_take)/gather | solution.py:59
  139.2 4.0 broadcast_select_fusion.1
  143.2 35.1 %reduce-scatter.6.cloned.1.call-done = bf16[128,2048]{1,0:T(8,128)(2,1)} async-done(((bf16[1024,2048]{1,0:T(8,128)(2,1)}), bf16[128,2048]{1,0:T(8,128)(2,1)}) %reduce-scatter.6.cloned.1.call-update) | async-done | bytes 524304 | tf_op jit(solution)/shard_map/reduce_scatter | solution.py:39
  178.4 37.8 %all-gather.2.cloned.1.call-done = bf16[1024,2048]{1,0:T(8,128)(2,1)} async-done(((bf16[128,2048]{1,0:T(8,128)(2,1)}), bf16[1024,2048]{1,0:T(8,128)(2,1)}) %all-gather.2.cloned.1.call-update) | async-done | bytes 4194320 | tf_op jit(solution)/shard_map/all_gather | solution.py:40
  216.2 13.5 %fusion.85 = f32[1024,1024]{0,1:T(8,128)} fusion(s32[]{:T(128)S(6)} %select_n.64, bf16[1024,2048]{1,0:T(8,128)(2,1)} %all-gather.2.cloned.1.call-done), kind=kOutput, calls=%fused_computation.182 | convolution fusion | flops 4303355904 | bytes 8388612 | tf_op jit(solution)/shard_map/dot_general | solution.py:77
  229.8 110.0 %all-reduce.4.cloned.1.call-done = f32[1024,1024]{0,1:T(8,128)} async-done(((f32[1024,1024]{0,1:T(8,128)}), f32[1024,1024]{0,1:T(8,128)}) %all-reduce.4.cloned.1.call-update) | async-done | bytes 4194320 | tf_op jit(solution)/shard_map/psum | solution.py:80
  342.1 2.4 fusion.2
  344.5 9.8 %fusion.11 = f32[1024,1024]{0,1:T(8,128)} fusion(bf16[1024,2048]{1,0:T(8,128)(2,1)S(1)} %copy-done.2, pred[1024]{0:T(1024)(128)(4,1)S(1)} %compare_and_fusion, s32[]{:T(128)S(6)} %select_n.64, bf16[1024,2048]{1,0:T(8,128)(2,1)} %all-gather.2.cloned.1.call-done), kind=kOutput, calls=%fused_computation.26 | convolution fusion | flops 4305453056 | bytes 12583940 | tf_op jit(solution)/shard_map/dot_general | solution.py:64
  354.4 84.2 %all-reduce.6.cloned.1.call-done = f32[1024,1024]{0,1:T(8,128)} async-done(((f32[1024,1024]{0,1:T(8,128)}), f32[1024,1024]{0,1:T(8,128)}) %all-reduce.6.cloned.1.call-update) | async-done | bytes 4194320 | tf_op jit(solution)/shard_map/psum | solution.py:80
  438.6 5.0 select_add_fusion
  443.6 5.4 copy.26
  449.0 4.5 fusion.1
  455.4 11.7 %cholesky.222 = f32[128,128]{1,0:T(8,128)S(1)} custom-call(f32[128,128]{1,0:T(8,128)S(1)} %cholesky.577), custom_call_target="Cholesky" | custom-call | tf_op jit(solution)/shard_map/jit(cholesky)/cholesky | solution.py:51
  467.3 9.8 %custom-call.62 = f32[1,128,128]{1,2,0:T(8,128)S(1)} custom-call(f32[1,128,128]{2,1,0:T(8,128)S(1)} %get-tuple-element.71), custom_call_target="InvertDiagBlocksLowerTriangular" | custom-call | tf_op jit(solution)/shard_map/jit(cholesky)/cholesky | solution.py:51
  480.4 11.7 %cholesky.243 = f32[128,128]{1,0:T(8,128)S(1)} custom-call(f32[128,128]{1,0:T(8,128)S(1)} %cholesky.581), custom_call_target="Cholesky" | custom-call | tf_op jit(solution)/shard_map/jit(cholesky)/cholesky | solution.py:51
  492.7 9.8 %custom-call.63 = f32[1,128,128]{1,2,0:T(8,128)S(1)} custom-call(f32[1,128,128]{2,1,0:T(8,128)S(1)} %get-tuple-element.69), custom_call_target="InvertDiagBlocksLowerTriangular" | custom-call | tf_op jit(solution)/shard_map/jit(cholesky)/cholesky | solution.py:51
  505.5 2.4 convolution_subtract_fusion.6
  508.0 11.7 %cholesky.466 = f32[128,128]{1,0:T(8,128)S(1)} custom-call(f32[128,128]{1,0:T(8,128)S(1)} %cholesky.586), custom_call_target="Cholesky" | custom-call | tf_op jit(solution)/shard_map/jit(cholesky)/cholesky | solution.py:51
  520.5 9.8 %custom-call.64 = f32[1,128,128]{1,2,0:T(8,128)S(1)} custom-call(f32[1,128,128]{2,1,0:T(8,128)S(1)} %get-tuple-element.67), custom_call_target="InvertDiagBlocksLowerTriangular" | custom-call | tf_op jit(solution)/shard_map/jit(cholesky)/cholesky | solution.py:51
  531.5 3.3 convolution_subtract_fusion.7
  534.8 11.7 %cholesky.485 = f32[128,128]{1,0:T(8,128)S(1)} custom-call(f32[128,128]{1,0:T(8,128)S(1)} %cholesky.591), custom_call_target="Cholesky" | custom-call | tf_op jit(solution)/shard_map/jit(cholesky)/cholesky | solution.py:51
  547.3 9.8 %custom-call.65 = f32[1,128,128]{1,2,0:T(8,128)S(1)} custom-call(f32[1,128,128]{2,1,0:T(8,128)S(1)} %get-tuple-element.65), custom_call_target="InvertDiagBlocksLowerTriangular" | custom-call | tf_op jit(solution)/shard_map/jit(cholesky)/cholesky | solution.py:51
  558.3 3.2 convolution_subtract_fusion.8
  561.4 12.1 %cholesky.504 = f32[128,128]{1,0:T(8,128)S(1)} custom-call(f32[128,128]{1,0:T(8,128)S(1)} %cholesky.596), custom_call_target="Cholesky" | custom-call | tf_op jit(solution)/shard_map/jit(cholesky)/cholesky | solution.py:51
  574.3 9.8 %custom-call.66 = f32[1,128,128]{1,2,0:T(8,128)S(1)} custom-call(f32[1,128,128]{2,1,0:T(8,128)S(1)} %get-tuple-element.63), custom_call_target="InvertDiagBlocksLowerTriangular" | custom-call | tf_op jit(solution)/shard_map/jit(cholesky)/cholesky | solution.py:51
  585.3 3.1 convolution_subtract_fusion.9
  588.4 11.7 %cholesky.524 = f32[128,128]{1,0:T(8,128)S(1)} custom-call(f32[128,128]{1,0:T(8,128)S(1)} %cholesky.601), custom_call_target="Cholesky" | custom-call | tf_op jit(solution)/shard_map/jit(cholesky)/cholesky | solution.py:51
  600.8 9.8 %custom-call.67 = f32[1,128,128]{1,2,0:T(8,128)S(1)} custom-call(f32[1,128,128]{2,1,0:T(8,128)S(1)} %get-tuple-element.61), custom_call_target="InvertDiagBlocksLowerTriangular" | custom-call | tf_op jit(solution)/shard_map/jit(cholesky)/cholesky | solution.py:51
  611.6 2.8 convolution_subtract_fusion.10
  614.5 11.7 %cholesky.544 = f32[128,128]{1,0:T(8,128)S(1)} custom-call(f32[128,128]{1,0:T(8,128)S(1)} %cholesky.606), custom_call_target="Cholesky" | custom-call | tf_op jit(solution)/shard_map/jit(cholesky)/cholesky | solution.py:51
  627.0 9.8 %custom-call.68 = f32[1,128,128]{1,2,0:T(8,128)S(1)} custom-call(f32[1,128,128]{2,1,0:T(8,128)S(1)} %get-tuple-element.59), custom_call_target="InvertDiagBlocksLowerTriangular" | custom-call | tf_op jit(solution)/shard_map/jit(cholesky)/cholesky | solution.py:51
  637.7 2.1 convolution_subtract_fusion.11
  639.8 11.7 %cholesky.562 = f32[128,128]{1,0:T(8,128)S(1)} custom-call(f32[128,128]{1,0:T(8,128)S(1)} %convolution_subtract_fusion.11), custom_call_target="Cholesky" | custom-call | tf_op jit(solution)/shard_map/jit(cholesky)/cholesky | solution.py:51
  661.9 4.9 select_select_fusion
  666.8 24.0 %while.1 = (s32[]{:T(128)}, f32[1024,1024]{0,1:T(8,128)}, s32[8,2]{0,1:T(2,128)S(1)}, f32[8,128,128]{2,1,0:T(8,128)S(1)}, s32[]{:T(128)}) while((s32[]{:T(128)}, f32[1024,1024]{0,1:T(8,128)}, s32[8,2]{0,1:T(2,128)S(1)}, f32[8,128,128]{2,1,0:T(8,128)S(1)}, s32[]{:T(128)}) %tuple.51), condition=%wide.while_cond, body=%wide.while_body.sunk | while | flops 2 | bytes 393329 | solution.py:52
  667.4 2.3 dynamic-slice.7
  670.4 2.3 dynamic-slice.7
  673.4 2.3 dynamic-slice.7
  676.4 2.3 dynamic-slice.7
  679.4 2.3 dynamic-slice.7
  682.4 2.3 dynamic-slice.7
  685.4 2.3 dynamic-slice.7
  688.4 2.2 dynamic-slice.7
  690.7 79.6 %custom-call.69 = f32[8,128,128]{1,2,0:T(8,128)} custom-call(f32[8,128,128]{2,1,0:T(8,128)S(1)} %get-tuple-element.14), custom_call_target="InvertDiagBlocksLowerTriangular" | custom-call | tf_op jit(solution)/shard_map/triangular_solve | solution.py:52
  770.4 2.5 constant_dynamic-update-slice_fusion.17
  772.9 2.1 convolution_subtract_fusion.4
  775.0 2.7 constant_dynamic-update-slice_fusion.16
  777.7 2.7 convolution_subtract_fusion
  782.2 3.7 fusion.18
  787.8 4.4 fusion.21
  794.1 5.4 convolution_subtract_fusion.2
  801.2 2.0 copy.50
  803.3 6.2 convolution_subtract_fusion.1
  809.5 2.5 constant_dynamic-update-slice_fusion.11
  812.0 8.5 %convolution_subtract_fusion.3 = f32[128,1024]{0,1:T(8,128)S(1)} fusion(f32[896,1024]{1,0:T(8,128)} %get-tuple-element.33, f32[1024,1024]{0,1:T(8,128)} %fusion.2, f32[1024,1024]{0,1:T(8,128)} %get-tuple-element.133), kind=kOutput, calls=%fused_computation.40 | convolution fusion | flops 1409417216 | bytes 5177344 | tf_op jit(solution)/shard_map/triangular_solve | solution.py:52
  820.5 2.3 convolution_dynamic-update-slice_fusion
  822.8 4.7 reduce-scatter.10.cloned.1.call-done
  828.7 7.6 fusion.33
  (119 shorter events, 41.9 us)
Async XLA Ops:
  7.8 21.0 %all-to-all-start = ((s32[32,1,32]{2,1,0:T(1,128)}), s32[32,1,32]{2,1,0:T(1,128)S(1)}, u32[]{:S(2)}, u32[]{:S(2)}) async-start(s32[32,1,32]{2,1,0:T(1,128)} %broadcast_in_dim.23), calls=%async_computation | async-start | bytes 32768 | tf_op jit(solution)/shard_map/all_to_all | solution.py:13
  28.8 98.8 %all-to-all-start.1 = ((bf16[32,32,2048]{2,0,1:T(8,128)(2,1)}), bf16[32,32,2048]{2,0,1:T(8,128)(2,1)}, u32[]{:S(2)}, u32[]{:S(2)}) async-start(bf16[32,32,2048]{2,0,1:T(8,128)(2,1)} %bitcast.117), calls=%async_computation.1 | async-start | bytes 8388608 | tf_op jit(solution)/shard_map/all_to_all | solution.py:56
  33.8 144.5 %reduce-scatter.6.cloned.1.call-start = ((), (), s32[]{:S(2)}) async-start(), calls=%async_computation.5 | async-start | bytes 4718592 | tf_op jit(solution)/shard_map/reduce_scatter | solution.py:39
  143.1 73.1 %all-gather.2.cloned.1.call-start = ((), (), s32[]{:S(2)}) async-start(), calls=%async_computation.6 | async-start | bytes 4718592 | tf_op jit(solution)/shard_map/all_gather | solution.py:40
  178.4 161.5 %all-reduce.4.cloned.1.call-start = ((), (), s32[]{:S(2)}) async-start(), calls=%async_computation.8 | async-start | bytes 8388608 | tf_op jit(solution)/shard_map/psum | solution.py:80
  229.7 208.9 %all-reduce.6.cloned.1.call-start = ((), (), s32[]{:S(2)}) async-start(), calls=%async_computation.9 | async-start | bytes 8388608 | tf_op jit(solution)/shard_map/psum | solution.py:80
  339.8 461.4 %reduce-scatter.8.cloned.1.call-start = ((), (), s32[]{:S(2)}) async-start(), calls=%async_computation.7 | async-start | bytes 4718592 | tf_op jit(solution)/shard_map/reduce_scatter | solution.py:46
  340.7 3.7 copy-start.2
  354.4 473.2 %reduce-scatter.10.cloned.1.call-start = ((), (), s32[]{:S(2)}) async-start(), calls=%async_computation.10 | async-start | bytes 655360
  453.5 2.0 copy-start.3
  503.6 2.0 copy-start
  770.3 7.4 copy-start.1
  772.9 7.6 copy-start.4
Sparse Core Ops, SparseCore 0:
  143.3 35.0 reduce-scatter.5
  180.2 35.9 all-gather.1
  229.9 109.9 all-reduce.3
  342.0 96.5 all-reduce.5
  441.0 55.2 reduce-scatter.7
  803.4 24.1 reduce-scatter.9
